TPU v7x, 256 devices: a whole 4x4x8 slice. The times are simulated.
256 devices in a mesh: blk: 16 (over x, z_lo, core), grp: 16 (over z_hi, y).
Axes of the slice: x: 4, y: 4, z: 8 (z_hi: 4, z_lo: 2; z = z_hi * 2 + z_lo), core: 2. Of those that a mesh axis runs over, the one named last changes fastest.
Arguments:
- amplitudes: bfloat16 [12288, 1024], P(('blk', 'grp')), may hold values from -6 to 6
- integrals: bfloat16 [1024, 65536], P(None, ('grp', 'blk')), may hold values from -0.1875 to 0.1875
- amplitude_mask: int32 [768, 8], P(('blk', 'grp')), may hold values 0 or 1
- integral_mask: int32 [8, 512], P(None, ('grp', 'blk')), may hold values 0 or 1
Outputs:
- residual: bfloat16 [12288, 65536], P('blk', 'grp')
All inputs are finite; a program needn't handle non-finite values. No bound on the sum of `amplitude_mask` or of `integral_mask` on one device may be relied on, other than what follows from the above.
Results may differ from a plain program's by a relative error of at most 0.001.
Values may be sent and summed in bfloat16 or wider, within the bound.
A program may use at most 64 MiB of HBM per device.

v0:
```python
import jax
import jax.numpy as jnp
from jax import lax
from jax.sharding import PartitionSpec as P

TILE = 128
OTILE = 16


def shifted(block, axis, distance):
    devices = range(lax.axis_size(axis))
    route = [((i - distance) % len(devices), i) for i in devices]
    return lax.ppermute(block, axis, route)


def mask_tiles(values, screen, row_tile, col_tile):
    height, breadth = values.shape
    tiled = values.reshape(height // row_tile, row_tile, breadth // col_tile, col_tile)
    tiled = tiled * screen.astype(values.dtype)[:, None, :, None]
    return tiled.reshape(height, breadth)


def local(amplitudes, integrals, amplitude_mask, integral_mask):
    amp_masked = mask_tiles(amplitudes, amplitude_mask, OTILE, TILE)
    int_panel = mask_tiles(integrals, integral_mask, TILE, TILE)
    gathered = lax.all_gather(amp_masked, "grp", axis=0, tiled=True)

    def contract(segment):
        return (0.5 * jnp.dot(gathered, segment, preferred_element_type=jnp.float32)).astype(
            jnp.bfloat16
        )

    cycle_size = lax.axis_size("blk")
    panel_width = int_panel.shape[1]
    position = lax.axis_index("blk")
    result = jnp.zeros((gathered.shape[0], cycle_size * panel_width), jnp.bfloat16)
    result = lax.dynamic_update_slice_in_dim(result, contract(int_panel), position * panel_width, 1)

    def advance(turn_index, carry):
        current, result = carry
        current = shifted(current, "blk", 1)
        owner = (position - turn_index) % cycle_size
        result = lax.dynamic_update_slice_in_dim(result, contract(current), owner * panel_width, 1)
        return (current, result)

    current, result = lax.fori_loop(1, cycle_size, advance, (int_panel, result))
    return result


def solution(mesh):
    return jax.shard_map(
        local,
        mesh=mesh,
        in_specs=(
            P(("blk", "grp"), None),
            P(None, ("grp", "blk")),
            P(("blk", "grp"), None),
            P(None, ("grp", "blk")),
        ),
        out_specs=P("blk", "grp"),
        check_vma=False,
    )
```

profile of v0, /device:TPU:8, one launch (start us, length us, event | category | flops | bytes accessed | tf_op | source)
XLA Modules:
  0.0 262.3 jit_solution(9153554101730459474)
XLA Ops:
  6.5 0.0 all-gather.2.cloned.1.call-start
  6.5 0.7 convert_element_type.20
  7.2 0.1 mul.51
  7.3 1.6 bitcast_multiply_fusion.1
  8.9 0.0 all-gather.2.cloned.1.call-update
  8.9 0.7 convert_element_type.19
  9.6 0.1 copy.5
  9.7 0.3 mul.48
  10.0 1.1 bitcast_multiply_fusion
  11.1 58.3 %all-gather.2.cloned.1.call-done = bf16[768,1024]{1,0:T(8,128)(2,1)} async-done(((bf16[48,1024]{1,0:T(8,128)(2,1)}), bf16[768,1024]{1,0:T(8,128)(2,1)}) %all-gather.2.cloned.1.call-update) | async-done | bytes 1572880 | tf_op jit(solution)/shard_map/all_gather | solution.py:26
  69.5 0.0 copy-start.1
  69.5 0.8 broadcast_in_dim.2
  70.3 0.6 copy-done.1
  70.9 0.6 fusion.3
  71.5 0.0 copy-start
  71.5 2.7 %copy-done = bf16[768,4096]{1,0:T(8,128)(2,1)} copy-done((bf16[768,4096]{1,0:T(8,128)(2,1)}, bf16[768,4096]{1,0:T(8,128)(2,1)S(1)}, u32[]{:S(2)}) %copy-start) | copy-done | bytes 6291480
  74.2 181.3 %while.17 = (s32[]{:T(128)}, bf16[1024,256]{1,0:T(8,128)(2,1)S(1)}, bf16[768,4096]{1,0:T(8,128)(2,1)}, bf16[768,1024]{1,0:T(8,128)(2,1)S(1)}, s32[]{:T(128)}, /*...) while((s32[]{:T(128)}, bf16[1024,256]{1,0:T(8,128)(2,1)S(1)}, ...), condition=%wide.region_1.2_spmd, body=%wide.region_0.1_spmd.sunk | while | flops 403046432 | bytes 5636416 | solution.py:46
  74.2 0.0 collective-permute-start
  74.2 10.7 %collective-permute-done = bf16[1024,256]{1,0:T(8,128)(2,1)S(1)} collective-permute-done((bf16[1024,256]{1,0:T(8,128)(2,1)S(1)}, bf16[1024,256]{1,0:T(8,128)(2,1)S(1)}, u32[]{:S(2)}, u32[]{:S(2)}) %collective-permute-start) | collective-permute-done | bytes 524320 | tf_op jit(solution)/shard_map/while/body/eval_jaxpr/ppermute | solution.py:13
  84.9 1.3 fusion.13
  86.3 0.0 collective-permute-start
  86.3 10.7 %collective-permute-done = bf16[1024,256]{1,0:T(8,128)(2,1)S(1)} collective-permute-done((bf16[1024,256]{1,0:T(8,128)(2,1)S(1)}, bf16[1024,256]{1,0:T(8,128)(2,1)S(1)}, u32[]{:S(2)}, u32[]{:S(2)}) %collective-permute-start) | collective-permute-done | bytes 524320 | tf_op jit(solution)/shard_map/while/body/eval_jaxpr/ppermute | solution.py:13
  97.0 1.3 fusion.13
  98.3 0.0 collective-permute-start
  98.3 10.7 %collective-permute-done = bf16[1024,256]{1,0:T(8,128)(2,1)S(1)} collective-permute-done((bf16[1024,256]{1,0:T(8,128)(2,1)S(1)}, bf16[1024,256]{1,0:T(8,128)(2,1)S(1)}, u32[]{:S(2)}, u32[]{:S(2)}) %collective-permute-start) | collective-permute-done | bytes 524320 | tf_op jit(solution)/shard_map/while/body/eval_jaxpr/ppermute | solution.py:13
  109.1 1.3 fusion.13
  110.4 0.0 collective-permute-start
  110.4 10.7 %collective-permute-done = bf16[1024,256]{1,0:T(8,128)(2,1)S(1)} collective-permute-done((bf16[1024,256]{1,0:T(8,128)(2,1)S(1)}, bf16[1024,256]{1,0:T(8,128)(2,1)S(1)}, u32[]{:S(2)}, u32[]{:S(2)}) %collective-permute-start) | collective-permute-done | bytes 524320 | tf_op jit(solution)/shard_map/while/body/eval_jaxpr/ppermute | solution.py:13
  121.2 1.3 fusion.13
  122.5 0.0 collective-permute-start
  122.5 10.7 %collective-permute-done = bf16[1024,256]{1,0:T(8,128)(2,1)S(1)} collective-permute-done((bf16[1024,256]{1,0:T(8,128)(2,1)S(1)}, bf16[1024,256]{1,0:T(8,128)(2,1)S(1)}, u32[]{:S(2)}, u32[]{:S(2)}) %collective-permute-start) | collective-permute-done | bytes 524320 | tf_op jit(solution)/shard_map/while/body/eval_jaxpr/ppermute | solution.py:13
  133.3 1.3 fusion.13
  134.6 0.0 collective-permute-start
  134.6 10.7 %collective-permute-done = bf16[1024,256]{1,0:T(8,128)(2,1)S(1)} collective-permute-done((bf16[1024,256]{1,0:T(8,128)(2,1)S(1)}, bf16[1024,256]{1,0:T(8,128)(2,1)S(1)}, u32[]{:S(2)}, u32[]{:S(2)}) %collective-permute-start) | collective-permute-done | bytes 524320 | tf_op jit(solution)/shard_map/while/body/eval_jaxpr/ppermute | solution.py:13
  145.3 1.3 fusion.13
  146.7 0.0 collective-permute-start
  146.7 10.7 %collective-permute-done = bf16[1024,256]{1,0:T(8,128)(2,1)S(1)} collective-permute-done((bf16[1024,256]{1,0:T(8,128)(2,1)S(1)}, bf16[1024,256]{1,0:T(8,128)(2,1)S(1)}, u32[]{:S(2)}, u32[]{:S(2)}) %collective-permute-start) | collective-permute-done | bytes 524320 | tf_op jit(solution)/shard_map/while/body/eval_jaxpr/ppermute | solution.py:13
  157.4 1.3 fusion.13
  158.8 0.0 collective-permute-start
  158.8 10.7 %collective-permute-done = bf16[1024,256]{1,0:T(8,128)(2,1)S(1)} collective-permute-done((bf16[1024,256]{1,0:T(8,128)(2,1)S(1)}, bf16[1024,256]{1,0:T(8,128)(2,1)S(1)}, u32[]{:S(2)}, u32[]{:S(2)}) %collective-permute-start) | collective-permute-done | bytes 524320 | tf_op jit(solution)/shard_map/while/body/eval_jaxpr/ppermute | solution.py:13
  169.5 1.3 fusion.13
  170.8 0.0 collective-permute-start
  170.8 10.7 %collective-permute-done = bf16[1024,256]{1,0:T(8,128)(2,1)S(1)} collective-permute-done((bf16[1024,256]{1,0:T(8,128)(2,1)S(1)}, bf16[1024,256]{1,0:T(8,128)(2,1)S(1)}, u32[]{:S(2)}, u32[]{:S(2)}) %collective-permute-start) | collective-permute-done | bytes 524320 | tf_op jit(solution)/shard_map/while/body/eval_jaxpr/ppermute | solution.py:13
  181.6 1.3 fusion.13
  182.9 0.0 collective-permute-start
  182.9 10.7 %collective-permute-done = bf16[1024,256]{1,0:T(8,128)(2,1)S(1)} collective-permute-done((bf16[1024,256]{1,0:T(8,128)(2,1)S(1)}, bf16[1024,256]{1,0:T(8,128)(2,1)S(1)}, u32[]{:S(2)}, u32[]{:S(2)}) %collective-permute-start) | collective-permute-done | bytes 524320 | tf_op jit(solution)/shard_map/while/body/eval_jaxpr/ppermute | solution.py:13
  193.7 1.3 fusion.13
  195.0 0.0 collective-permute-start
  195.0 10.7 %collective-permute-done = bf16[1024,256]{1,0:T(8,128)(2,1)S(1)} collective-permute-done((bf16[1024,256]{1,0:T(8,128)(2,1)S(1)}, bf16[1024,256]{1,0:T(8,128)(2,1)S(1)}, u32[]{:S(2)}, u32[]{:S(2)}) %collective-permute-start) | collective-permute-done | bytes 524320 | tf_op jit(solution)/shard_map/while/body/eval_jaxpr/ppermute | solution.py:13
  205.8 1.3 fusion.13
  207.1 0.0 collective-permute-start
  207.1 10.7 %collective-permute-done = bf16[1024,256]{1,0:T(8,128)(2,1)S(1)} collective-permute-done((bf16[1024,256]{1,0:T(8,128)(2,1)S(1)}, bf16[1024,256]{1,0:T(8,128)(2,1)S(1)}, u32[]{:S(2)}, u32[]{:S(2)}) %collective-permute-start) | collective-permute-done | bytes 524320 | tf_op jit(solution)/shard_map/while/body/eval_jaxpr/ppermute | solution.py:13
  217.8 1.3 fusion.13
  219.2 0.0 collective-permute-start
  219.2 10.7 %collective-permute-done = bf16[1024,256]{1,0:T(8,128)(2,1)S(1)} collective-permute-done((bf16[1024,256]{1,0:T(8,128)(2,1)S(1)}, bf16[1024,256]{1,0:T(8,128)(2,1)S(1)}, u32[]{:S(2)}, u32[]{:S(2)}) %collective-permute-start) | collective-permute-done | bytes 524320 | tf_op jit(solution)/shard_map/while/body/eval_jaxpr/ppermute | solution.py:13
  229.9 1.3 fusion.13
  231.3 0.0 collective-permute-start
  231.3 10.7 %collective-permute-done = bf16[1024,256]{1,0:T(8,128)(2,1)S(1)} collective-permute-done((bf16[1024,256]{1,0:T(8,128)(2,1)S(1)}, bf16[1024,256]{1,0:T(8,128)(2,1)S(1)}, u32[]{:S(2)}, u32[]{:S(2)}) %collective-permute-start) | collective-permute-done | bytes 524320 | tf_op jit(solution)/shard_map/while/body/eval_jaxpr/ppermute | solution.py:13
  242.0 1.3 fusion.13
  243.3 0.0 collective-permute-start
  243.3 10.7 %collective-permute-done = bf16[1024,256]{1,0:T(8,128)(2,1)S(1)} collective-permute-done((bf16[1024,256]{1,0:T(8,128)(2,1)S(1)}, bf16[1024,256]{1,0:T(8,128)(2,1)S(1)}, u32[]{:S(2)}, u32[]{:S(2)}) %collective-permute-start) | collective-permute-done | bytes 524320 | tf_op jit(solution)/shard_map/while/body/eval_jaxpr/ppermute | solution.py:13
  254.1 1.3 fusion.13
  (15 shorter events, 0.5 us)
Async XLA Ops:
  6.5 62.9 %all-gather.2.cloned.1.call-start = ((), (), s32[]{:S(2)}) async-start(), calls=%async_computation | async-start | bytes 1671168 | tf_op jit(solution)/shard_map/all_gather | solution.py:26
  69.5 1.4 copy-start.1
  71.5 2.7 %copy-start = (bf16[768,4096]{1,0:T(8,128)(2,1)}, bf16[768,4096]{1,0:T(8,128)(2,1)S(1)}, u32[]{:S(2)}) copy-start(bf16[768,4096]{1,0:T(8,128)(2,1)S(1)} %fusion.3) | copy-start | bytes 18874372
  74.2 10.7 %collective-permute-start = (bf16[1024,256]{1,0:T(8,128)(2,1)S(1)}, bf16[1024,256]{1,0:T(8,128)(2,1)S(1)}, u32[]{:S(2)}, u32[]{:S(2)}) collective-permute-start(bf16[1024,256]{1,0:T(8,128)(2,1)S(1)} %get-tuple-element.192), channel_id=1, source_target_pairs={{240,0},{0,16},{16,32},{32,48},{48,64},{64,80},{80,96},{96,112},{1... | collective-permute-start | bytes 1572872 | tf_op jit(solution)/shard_map/while/body/eval_jaxpr/ppermute | solution.py:13
  86.3 10.7 %collective-permute-start = (bf16[1024,256]{1,0:T(8,128)(2,1)S(1)}, bf16[1024,256]{1,0:T(8,128)(2,1)S(1)}, u32[]{:S(2)}, u32[]{:S(2)}) collective-permute-start(bf16[1024,256]{1,0:T(8,128)(2,1)S(1)} %get-tuple-element.192), channel_id=1, source_target_pairs={{240,0},{0,16},{16,32},{32,48},{48,64},{64,80},{80,96},{96,112},{1... | collective-permute-start | bytes 1572872 | tf_op jit(solution)/shard_map/while/body/eval_jaxpr/ppermute | solution.py:13
  98.3 10.7 %collective-permute-start = (bf16[1024,256]{1,0:T(8,128)(2,1)S(1)}, bf16[1024,256]{1,0:T(8,128)(2,1)S(1)}, u32[]{:S(2)}, u32[]{:S(2)}) collective-permute-start(bf16[1024,256]{1,0:T(8,128)(2,1)S(1)} %get-tuple-element.192), channel_id=1, source_target_pairs={{240,0},{0,16},{16,32},{32,48},{48,64},{64,80},{80,96},{96,112},{1... | collective-permute-start | bytes 1572872 | tf_op jit(solution)/shard_map/while/body/eval_jaxpr/ppermute | solution.py:13
  110.4 10.7 %collective-permute-start = (bf16[1024,256]{1,0:T(8,128)(2,1)S(1)}, bf16[1024,256]{1,0:T(8,128)(2,1)S(1)}, u32[]{:S(2)}, u32[]{:S(2)}) collective-permute-start(bf16[1024,256]{1,0:T(8,128)(2,1)S(1)} %get-tuple-element.192), channel_id=1, source_target_pairs={{240,0},{0,16},{16,32},{32,48},{48,64},{64,80},{80,96},{96,112},{1... | collective-permute-start | bytes 1572872 | tf_op jit(solution)/shard_map/while/body/eval_jaxpr/ppermute | solution.py:13
  122.5 10.7 %collective-permute-start = (bf16[1024,256]{1,0:T(8,128)(2,1)S(1)}, bf16[1024,256]{1,0:T(8,128)(2,1)S(1)}, u32[]{:S(2)}, u32[]{:S(2)}) collective-permute-start(bf16[1024,256]{1,0:T(8,128)(2,1)S(1)} %get-tuple-element.192), channel_id=1, source_target_pairs={{240,0},{0,16},{16,32},{32,48},{48,64},{64,80},{80,96},{96,112},{1... | collective-permute-start | bytes 1572872 | tf_op jit(solution)/shard_map/while/body/eval_jaxpr/ppermute | solution.py:13
  134.6 10.7 %collective-permute-start = (bf16[1024,256]{1,0:T(8,128)(2,1)S(1)}, bf16[1024,256]{1,0:T(8,128)(2,1)S(1)}, u32[]{:S(2)}, u32[]{:S(2)}) collective-permute-start(bf16[1024,256]{1,0:T(8,128)(2,1)S(1)} %get-tuple-element.192), channel_id=1, source_target_pairs={{240,0},{0,16},{16,32},{32,48},{48,64},{64,80},{80,96},{96,112},{1... | collective-permute-start | bytes 1572872 | tf_op jit(solution)/shard_map/while/body/eval_jaxpr/ppermute | solution.py:13
  146.7 10.7 %collective-permute-start = (bf16[1024,256]{1,0:T(8,128)(2,1)S(1)}, bf16[1024,256]{1,0:T(8,128)(2,1)S(1)}, u32[]{:S(2)}, u32[]{:S(2)}) collective-permute-start(bf16[1024,256]{1,0:T(8,128)(2,1)S(1)} %get-tuple-element.192), channel_id=1, source_target_pairs={{240,0},{0,16},{16,32},{32,48},{48,64},{64,80},{80,96},{96,112},{1... | collective-permute-start | bytes 1572872 | tf_op jit(solution)/shard_map/while/body/eval_jaxpr/ppermute | solution.py:13
  158.8 10.7 %collective-permute-start = (bf16[1024,256]{1,0:T(8,128)(2,1)S(1)}, bf16[1024,256]{1,0:T(8,128)(2,1)S(1)}, u32[]{:S(2)}, u32[]{:S(2)}) collective-permute-start(bf16[1024,256]{1,0:T(8,128)(2,1)S(1)} %get-tuple-element.192), channel_id=1, source_target_pairs={{240,0},{0,16},{16,32},{32,48},{48,64},{64,80},{80,96},{96,112},{1... | collective-permute-start | bytes 1572872 | tf_op jit(solution)/shard_map/while/body/eval_jaxpr/ppermute | solution.py:13
  170.8 10.7 %collective-permute-start = (bf16[1024,256]{1,0:T(8,128)(2,1)S(1)}, bf16[1024,256]{1,0:T(8,128)(2,1)S(1)}, u32[]{:S(2)}, u32[]{:S(2)}) collective-permute-start(bf16[1024,256]{1,0:T(8,128)(2,1)S(1)} %get-tuple-element.192), channel_id=1, source_target_pairs={{240,0},{0,16},{16,32},{32,48},{48,64},{64,80},{80,96},{96,112},{1... | collective-permute-start | bytes 1572872 | tf_op jit(solution)/shard_map/while/body/eval_jaxpr/ppermute | solution.py:13
  182.9 10.7 %collective-permute-start = (bf16[1024,256]{1,0:T(8,128)(2,1)S(1)}, bf16[1024,256]{1,0:T(8,128)(2,1)S(1)}, u32[]{:S(2)}, u32[]{:S(2)}) collective-permute-start(bf16[1024,256]{1,0:T(8,128)(2,1)S(1)} %get-tuple-element.192), channel_id=1, source_target_pairs={{240,0},{0,16},{16,32},{32,48},{48,64},{64,80},{80,96},{96,112},{1... | collective-permute-start | bytes 1572872 | tf_op jit(solution)/shard_map/while/body/eval_jaxpr/ppermute | solution.py:13
  195.0 10.7 %collective-permute-start = (bf16[1024,256]{1,0:T(8,128)(2,1)S(1)}, bf16[1024,256]{1,0:T(8,128)(2,1)S(1)}, u32[]{:S(2)}, u32[]{:S(2)}) collective-permute-start(bf16[1024,256]{1,0:T(8,128)(2,1)S(1)} %get-tuple-element.192), channel_id=1, source_target_pairs={{240,0},{0,16},{16,32},{32,48},{48,64},{64,80},{80,96},{96,112},{1... | collective-permute-start | bytes 1572872 | tf_op jit(solution)/shard_map/while/body/eval_jaxpr/ppermute | solution.py:13
  207.1 10.7 %collective-permute-start = (bf16[1024,256]{1,0:T(8,128)(2,1)S(1)}, bf16[1024,256]{1,0:T(8,128)(2,1)S(1)}, u32[]{:S(2)}, u32[]{:S(2)}) collective-permute-start(bf16[1024,256]{1,0:T(8,128)(2,1)S(1)} %get-tuple-element.192), channel_id=1, source_target_pairs={{240,0},{0,16},{16,32},{32,48},{48,64},{64,80},{80,96},{96,112},{1... | collective-permute-start | bytes 1572872 | tf_op jit(solution)/shard_map/while/body/eval_jaxpr/ppermute | solution.py:13
  219.2 10.7 %collective-permute-start = (bf16[1024,256]{1,0:T(8,128)(2,1)S(1)}, bf16[1024,256]{1,0:T(8,128)(2,1)S(1)}, u32[]{:S(2)}, u32[]{:S(2)}) collective-permute-start(bf16[1024,256]{1,0:T(8,128)(2,1)S(1)} %get-tuple-element.192), channel_id=1, source_target_pairs={{240,0},{0,16},{16,32},{32,48},{48,64},{64,80},{80,96},{96,112},{1... | collective-permute-start | bytes 1572872 | tf_op jit(solution)/shard_map/while/body/eval_jaxpr/ppermute | solution.py:13
  231.3 10.7 %collective-permute-start = (bf16[1024,256]{1,0:T(8,128)(2,1)S(1)}, bf16[1024,256]{1,0:T(8,128)(2,1)S(1)}, u32[]{:S(2)}, u32[]{:S(2)}) collective-permute-start(bf16[1024,256]{1,0:T(8,128)(2,1)S(1)} %get-tuple-element.192), channel_id=1, source_target_pairs={{240,0},{0,16},{16,32},{32,48},{48,64},{64,80},{80,96},{96,112},{1... | collective-permute-start | bytes 1572872 | tf_op jit(solution)/shard_map/while/body/eval_jaxpr/ppermute | solution.py:13
  243.3 10.7 %collective-permute-start = (bf16[1024,256]{1,0:T(8,128)(2,1)S(1)}, bf16[1024,256]{1,0:T(8,128)(2,1)S(1)}, u32[]{:S(2)}, u32[]{:S(2)}) collective-permute-start(bf16[1024,256]{1,0:T(8,128)(2,1)S(1)} %get-tuple-element.192), channel_id=1, source_target_pairs={{240,0},{0,16},{16,32},{32,48},{48,64},{64,80},{80,96},{96,112},{1... | collective-permute-start | bytes 1572872 | tf_op jit(solution)/shard_map/while/body/eval_jaxpr/ppermute | solution.py:13
Sparse Core Ops, SparseCore 0:
  9.8 59.6 all-gather.1
where the time goes:
time: 262 us
  waiting for transfers between devices  219 us (84%)
  matrix products  20.5 us (8%)
  between operations  13.4 us (5%)
  local copies, waits for them, and re-layouts  5.14 us (2%)
  other arithmetic  4.04 us (2%)
    ppermute x15, waiting for transfers between devices, shifted(): return lax.ppermute(block, axis, route)  161 us
    all_gather x1, waiting for transfers between devices, local(): gathered = lax.all_gather(amp_masked, 'grp', axis=0, tiled=True)  58.3 us
    dot_general x16, matrix products, contract(): jnp.dot(gathered, segment, preferred_element_type=jnp.float32)  20.5 us
  transfers between devices with their start and end apart: 16, of which 16 were waited for; matrix products, arithmetic and copies ran while one was open for 1% of the time, Pallas kernels for 0%

commit v1 on v0

--- a/solution.py
+++ b/solution.py
@@ -23,7 +23,8 @@
 def local(amplitudes, integrals, amplitude_mask, integral_mask):
     amp_masked = mask_tiles(amplitudes, amplitude_mask, OTILE, TILE)
     int_panel = mask_tiles(integrals, integral_mask, TILE, TILE)
-    gathered = lax.all_gather(amp_masked, "grp", axis=0, tiled=True)
+    stack = jnp.stack([amp_masked] * lax.axis_size("grp"))
+    gathered = jnp.concatenate(lax.all_to_all(stack, "grp", 0, 0), axis=0)
 
     def contract(segment):
         return (0.5 * jnp.dot(gathered, segment, preferred_element_type=jnp.float32)).astype(

time: 262 us -> 238 us (0.908)
  waiting for transfers between devices: 219 us -> 196 us
  between operations: 13.4 us -> 0.05 us
  starting transfers between devices: 0.04 us -> 11.6 us
    all_gather x1 -> x0, waiting for transfers between devices: 58.3 us -> none  [local(): gathered = lax.all_gather(amp_masked, 'grp', axis=0, tiled=True)]
    all_to_all x0 -> x1, waiting for transfers between devices: none -> 35.6 us  [local(): gathered = jnp.concatenate(lax.all_to_all(stack, 'grp', 0, 0), axis=0)]
    all_to_all x0 -> x1, starting transfers between devices: none -> 11.6 us  [local(): gathered = jnp.concatenate(lax.all_to_all(stack, 'grp', 0, 0), axis=0)]
where the time goes in v1:
time: 238 us
  waiting for transfers between devices  196 us (82%)
  matrix products  20.5 us (9%)
  starting transfers between devices  11.6 us (5%)
  local copies, waits for them, and re-layouts  5.84 us (2%)
  other arithmetic  3.39 us (1%)
    ppermute x15, waiting for transfers between devices, shifted(): return lax.ppermute(block, axis, route)  161 us
    all_to_all x1, waiting for transfers between devices, local(): gathered = jnp.concatenate(lax.all_to_all(stack, 'grp', 0, 0), axis=0)  35.6 us
    dot_general x16, matrix products, contract(): jnp.dot(gathered, segment, preferred_element_type=jnp.float32)  20.5 us
    all_to_all x1, starting transfers between devices, local(): gathered = jnp.concatenate(lax.all_to_all(stack, 'grp', 0, 0), axis=0)  11.6 us
  transfers between devices with their start and end apart: 16, of which 16 were waited for; matrix products, arithmetic and copies ran while one was open for 1% of the time, Pallas kernels for 0%

profile of v1, /device:TPU:8, one launch (start us, length us, event | category | flops | bytes accessed | tf_op | source)
XLA Modules:
  0.0 237.8 jit_solution(18238542595412137596)
XLA Ops:
  0.0 0.7 convert_element_type.20
  0.7 0.1 mul.52
  0.8 0.9 bitcast_multiply_fusion.1
  1.7 1.3 stack.3
  3.0 11.6 %all-to-all-start = ((bf16[16,48,1024]{2,1,0:T(8,128)(2,1)}), bf16[16,48,1024]{2,1,0:T(8,128)(2,1)S(1)}, u32[]{:S(2)}, u32[]{:S(2)}) async-start(bf16[16,48,1024]{2,1,0:T(8,128)(2,1)} %stack.3), calls=%async_computation | async-start | bytes 3145728 | tf_op jit(solution)/shard_map/all_to_all | solution.py:27
  14.6 0.7 convert_element_type.19
  15.3 0.1 copy.5
  15.4 0.3 mul.49
  15.7 1.1 bitcast_multiply_fusion
  16.8 35.6 %all-to-all-done = bf16[16,48,1024]{2,1,0:T(8,128)(2,1)S(1)} async-done(((bf16[16,48,1024]{2,1,0:T(8,128)(2,1)}), bf16[16,48,1024]{2,1,0:T(8,128)(2,1)S(1)}, u32[]{:S(2)}, u32[]{:S(2)}) %all-to-all-start) | async-done | bytes 1572896 | tf_op jit(solution)/shard_map/all_to_all | solution.py:27
  52.4 0.8 broadcast_in_dim.2
  53.2 0.6 fusion.3
  53.8 0.0 copy-start
  53.8 2.7 %copy-done = bf16[768,4096]{1,0:T(8,128)(2,1)} copy-done((bf16[768,4096]{1,0:T(8,128)(2,1)}, bf16[768,4096]{1,0:T(8,128)(2,1)S(1)}, u32[]{:S(2)}) %copy-start) | copy-done | bytes 6291480
  56.5 181.3 %while.17 = (s32[]{:T(128)}, bf16[1024,256]{1,0:T(8,128)(2,1)S(1)}, bf16[768,4096]{1,0:T(8,128)(2,1)}, bf16[768,1024]{1,0:T(8,128)(2,1)S(1)}, s32[]{:T(128)}, /*...) while((s32[]{:T(128)}, bf16[1024,256]{1,0:T(8,128)(2,1)S(1)}, ...), condition=%wide.region_1.2_spmd, body=%wide.region_0.1_spmd.sunk | while | flops 403046432 | bytes 5636416 | solution.py:47
  56.5 0.0 collective-permute-start
  56.5 10.7 %collective-permute-done = bf16[1024,256]{1,0:T(8,128)(2,1)S(1)} collective-permute-done((bf16[1024,256]{1,0:T(8,128)(2,1)S(1)}, bf16[1024,256]{1,0:T(8,128)(2,1)S(1)}, u32[]{:S(2)}, u32[]{:S(2)}) %collective-permute-start) | collective-permute-done | bytes 524320 | tf_op jit(solution)/shard_map/while/body/eval_jaxpr/ppermute | solution.py:13
  67.2 1.3 fusion.13
  68.6 0.0 collective-permute-start
  68.6 10.7 %collective-permute-done = bf16[1024,256]{1,0:T(8,128)(2,1)S(1)} collective-permute-done((bf16[1024,256]{1,0:T(8,128)(2,1)S(1)}, bf16[1024,256]{1,0:T(8,128)(2,1)S(1)}, u32[]{:S(2)}, u32[]{:S(2)}) %collective-permute-start) | collective-permute-done | bytes 524320 | tf_op jit(solution)/shard_map/while/body/eval_jaxpr/ppermute | solution.py:13
  79.3 1.3 fusion.13
  80.7 0.0 collective-permute-start
  80.7 10.7 %collective-permute-done = bf16[1024,256]{1,0:T(8,128)(2,1)S(1)} collective-permute-done((bf16[1024,256]{1,0:T(8,128)(2,1)S(1)}, bf16[1024,256]{1,0:T(8,128)(2,1)S(1)}, u32[]{:S(2)}, u32[]{:S(2)}) %collective-permute-start) | collective-permute-done | bytes 524320 | tf_op jit(solution)/shard_map/while/body/eval_jaxpr/ppermute | solution.py:13
  91.4 1.3 fusion.13
  92.7 0.0 collective-permute-start
  92.7 10.7 %collective-permute-done = bf16[1024,256]{1,0:T(8,128)(2,1)S(1)} collective-permute-done((bf16[1024,256]{1,0:T(8,128)(2,1)S(1)}, bf16[1024,256]{1,0:T(8,128)(2,1)S(1)}, u32[]{:S(2)}, u32[]{:S(2)}) %collective-permute-start) | collective-permute-done | bytes 524320 | tf_op jit(solution)/shard_map/while/body/eval_jaxpr/ppermute | solution.py:13
  103.5 1.3 fusion.13
  104.8 0.0 collective-permute-start
  104.8 10.7 %collective-permute-done = bf16[1024,256]{1,0:T(8,128)(2,1)S(1)} collective-permute-done((bf16[1024,256]{1,0:T(8,128)(2,1)S(1)}, bf16[1024,256]{1,0:T(8,128)(2,1)S(1)}, u32[]{:S(2)}, u32[]{:S(2)}) %collective-permute-start) | collective-permute-done | bytes 524320 | tf_op jit(solution)/shard_map/while/body/eval_jaxpr/ppermute | solution.py:13
  115.6 1.3 fusion.13
  116.9 0.0 collective-permute-start
  116.9 10.7 %collective-permute-done = bf16[1024,256]{1,0:T(8,128)(2,1)S(1)} collective-permute-done((bf16[1024,256]{1,0:T(8,128)(2,1)S(1)}, bf16[1024,256]{1,0:T(8,128)(2,1)S(1)}, u32[]{:S(2)}, u32[]{:S(2)}) %collective-permute-start) | collective-permute-done | bytes 524320 | tf_op jit(solution)/shard_map/while/body/eval_jaxpr/ppermute | solution.py:13
  127.7 1.3 fusion.13
  129.0 0.0 collective-permute-start
  129.0 10.7 %collective-permute-done = bf16[1024,256]{1,0:T(8,128)(2,1)S(1)} collective-permute-done((bf16[1024,256]{1,0:T(8,128)(2,1)S(1)}, bf16[1024,256]{1,0:T(8,128)(2,1)S(1)}, u32[]{:S(2)}, u32[]{:S(2)}) %collective-permute-start) | collective-permute-done | bytes 524320 | tf_op jit(solution)/shard_map/while/body/eval_jaxpr/ppermute | solution.py:13
  139.7 1.3 fusion.13
  141.1 0.0 collective-permute-start
  141.1 10.7 %collective-permute-done = bf16[1024,256]{1,0:T(8,128)(2,1)S(1)} collective-permute-done((bf16[1024,256]{1,0:T(8,128)(2,1)S(1)}, bf16[1024,256]{1,0:T(8,128)(2,1)S(1)}, u32[]{:S(2)}, u32[]{:S(2)}) %collective-permute-start) | collective-permute-done | bytes 524320 | tf_op jit(solution)/shard_map/while/body/eval_jaxpr/ppermute | solution.py:13
  151.8 1.3 fusion.13
  153.2 0.0 collective-permute-start
  153.2 10.7 %collective-permute-done = bf16[1024,256]{1,0:T(8,128)(2,1)S(1)} collective-permute-done((bf16[1024,256]{1,0:T(8,128)(2,1)S(1)}, bf16[1024,256]{1,0:T(8,128)(2,1)S(1)}, u32[]{:S(2)}, u32[]{:S(2)}) %collective-permute-start) | collective-permute-done | bytes 524320 | tf_op jit(solution)/shard_map/while/body/eval_jaxpr/ppermute | solution.py:13
  163.9 1.3 fusion.13
  165.2 0.0 collective-permute-start
  165.3 10.7 %collective-permute-done = bf16[1024,256]{1,0:T(8,128)(2,1)S(1)} collective-permute-done((bf16[1024,256]{1,0:T(8,128)(2,1)S(1)}, bf16[1024,256]{1,0:T(8,128)(2,1)S(1)}, u32[]{:S(2)}, u32[]{:S(2)}) %collective-permute-start) | collective-permute-done | bytes 524320 | tf_op jit(solution)/shard_map/while/body/eval_jaxpr/ppermute | solution.py:13
  176.0 1.3 fusion.13
  177.3 0.0 collective-permute-start
  177.3 10.7 %collective-permute-done = bf16[1024,256]{1,0:T(8,128)(2,1)S(1)} collective-permute-done((bf16[1024,256]{1,0:T(8,128)(2,1)S(1)}, bf16[1024,256]{1,0:T(8,128)(2,1)S(1)}, u32[]{:S(2)}, u32[]{:S(2)}) %collective-permute-start) | collective-permute-done | bytes 524320 | tf_op jit(solution)/shard_map/while/body/eval_jaxpr/ppermute | solution.py:13
  188.1 1.3 fusion.13
  189.4 0.0 collective-permute-start
  189.4 10.7 %collective-permute-done = bf16[1024,256]{1,0:T(8,128)(2,1)S(1)} collective-permute-done((bf16[1024,256]{1,0:T(8,128)(2,1)S(1)}, bf16[1024,256]{1,0:T(8,128)(2,1)S(1)}, u32[]{:S(2)}, u32[]{:S(2)}) %collective-permute-start) | collective-permute-done | bytes 524320 | tf_op jit(solution)/shard_map/while/body/eval_jaxpr/ppermute | solution.py:13
  200.2 1.3 fusion.13
  201.5 0.0 collective-permute-start
  201.5 10.7 %collective-permute-done = bf16[1024,256]{1,0:T(8,128)(2,1)S(1)} collective-permute-done((bf16[1024,256]{1,0:T(8,128)(2,1)S(1)}, bf16[1024,256]{1,0:T(8,128)(2,1)S(1)}, u32[]{:S(2)}, u32[]{:S(2)}) %collective-permute-start) | collective-permute-done | bytes 524320 | tf_op jit(solution)/shard_map/while/body/eval_jaxpr/ppermute | solution.py:13
  212.3 1.3 fusion.13
  213.6 0.0 collective-permute-start
  213.6 10.7 %collective-permute-done = bf16[1024,256]{1,0:T(8,128)(2,1)S(1)} collective-permute-done((bf16[1024,256]{1,0:T(8,128)(2,1)S(1)}, bf16[1024,256]{1,0:T(8,128)(2,1)S(1)}, u32[]{:S(2)}, u32[]{:S(2)}) %collective-permute-start) | collective-permute-done | bytes 524320 | tf_op jit(solution)/shard_map/while/body/eval_jaxpr/ppermute | solution.py:13
  224.3 1.3 fusion.13
  225.7 0.0 collective-permute-start
  225.7 10.7 %collective-permute-done = bf16[1024,256]{1,0:T(8,128)(2,1)S(1)} collective-permute-done((bf16[1024,256]{1,0:T(8,128)(2,1)S(1)}, bf16[1024,256]{1,0:T(8,128)(2,1)S(1)}, u32[]{:S(2)}, u32[]{:S(2)}) %collective-permute-start) | collective-permute-done | bytes 524320 | tf_op jit(solution)/shard_map/while/body/eval_jaxpr/ppermute | solution.py:13
  236.4 1.3 fusion.13
  (15 shorter events, 0.5 us)
Async XLA Ops:
  3.0 49.4 %all-to-all-start = ((bf16[16,48,1024]{2,1,0:T(8,128)(2,1)}), bf16[16,48,1024]{2,1,0:T(8,128)(2,1)S(1)}, u32[]{:S(2)}, u32[]{:S(2)}) async-start(bf16[16,48,1024]{2,1,0:T(8,128)(2,1)} %stack.3), calls=%async_computation | async-start | bytes 3145728 | tf_op jit(solution)/shard_map/all_to_all | solution.py:27
  53.8 2.7 %copy-start = (bf16[768,4096]{1,0:T(8,128)(2,1)}, bf16[768,4096]{1,0:T(8,128)(2,1)S(1)}, u32[]{:S(2)}) copy-start(bf16[768,4096]{1,0:T(8,128)(2,1)S(1)} %fusion.3) | copy-start | bytes 18874372
  56.5 10.7 %collective-permute-start = (bf16[1024,256]{1,0:T(8,128)(2,1)S(1)}, bf16[1024,256]{1,0:T(8,128)(2,1)S(1)}, u32[]{:S(2)}, u32[]{:S(2)}) collective-permute-start(bf16[1024,256]{1,0:T(8,128)(2,1)S(1)} %get-tuple-element.192), channel_id=1, source_target_pairs={{240,0},{0,16},{16,32},{32,48},{48,64},{64,80},{80,96},{96,112},{1... | collective-permute-start | bytes 1572872 | tf_op jit(solution)/shard_map/while/body/eval_jaxpr/ppermute | solution.py:13
  68.6 10.7 %collective-permute-start = (bf16[1024,256]{1,0:T(8,128)(2,1)S(1)}, bf16[1024,256]{1,0:T(8,128)(2,1)S(1)}, u32[]{:S(2)}, u32[]{:S(2)}) collective-permute-start(bf16[1024,256]{1,0:T(8,128)(2,1)S(1)} %get-tuple-element.192), channel_id=1, source_target_pairs={{240,0},{0,16},{16,32},{32,48},{48,64},{64,80},{80,96},{96,112},{1... | collective-permute-start | bytes 1572872 | tf_op jit(solution)/shard_map/while/body/eval_jaxpr/ppermute | solution.py:13
  80.7 10.7 %collective-permute-start = (bf16[1024,256]{1,0:T(8,128)(2,1)S(1)}, bf16[1024,256]{1,0:T(8,128)(2,1)S(1)}, u32[]{:S(2)}, u32[]{:S(2)}) collective-permute-start(bf16[1024,256]{1,0:T(8,128)(2,1)S(1)} %get-tuple-element.192), channel_id=1, source_target_pairs={{240,0},{0,16},{16,32},{32,48},{48,64},{64,80},{80,96},{96,112},{1... | collective-permute-start | bytes 1572872 | tf_op jit(solution)/shard_map/while/body/eval_jaxpr/ppermute | solution.py:13
  92.7 10.7 %collective-permute-start = (bf16[1024,256]{1,0:T(8,128)(2,1)S(1)}, bf16[1024,256]{1,0:T(8,128)(2,1)S(1)}, u32[]{:S(2)}, u32[]{:S(2)}) collective-permute-start(bf16[1024,256]{1,0:T(8,128)(2,1)S(1)} %get-tuple-element.192), channel_id=1, source_target_pairs={{240,0},{0,16},{16,32},{32,48},{48,64},{64,80},{80,96},{96,112},{1... | collective-permute-start | bytes 1572872 | tf_op jit(solution)/shard_map/while/body/eval_jaxpr/ppermute | solution.py:13
  104.8 10.7 %collective-permute-start = (bf16[1024,256]{1,0:T(8,128)(2,1)S(1)}, bf16[1024,256]{1,0:T(8,128)(2,1)S(1)}, u32[]{:S(2)}, u32[]{:S(2)}) collective-permute-start(bf16[1024,256]{1,0:T(8,128)(2,1)S(1)} %get-tuple-element.192), channel_id=1, source_target_pairs={{240,0},{0,16},{16,32},{32,48},{48,64},{64,80},{80,96},{96,112},{1... | collective-permute-start | bytes 1572872 | tf_op jit(solution)/shard_map/while/body/eval_jaxpr/ppermute | solution.py:13
  116.9 10.7 %collective-permute-start = (bf16[1024,256]{1,0:T(8,128)(2,1)S(1)}, bf16[1024,256]{1,0:T(8,128)(2,1)S(1)}, u32[]{:S(2)}, u32[]{:S(2)}) collective-permute-start(bf16[1024,256]{1,0:T(8,128)(2,1)S(1)} %get-tuple-element.192), channel_id=1, source_target_pairs={{240,0},{0,16},{16,32},{32,48},{48,64},{64,80},{80,96},{96,112},{1... | collective-permute-start | bytes 1572872 | tf_op jit(solution)/shard_map/while/body/eval_jaxpr/ppermute | solution.py:13
  129.0 10.7 %collective-permute-start = (bf16[1024,256]{1,0:T(8,128)(2,1)S(1)}, bf16[1024,256]{1,0:T(8,128)(2,1)S(1)}, u32[]{:S(2)}, u32[]{:S(2)}) collective-permute-start(bf16[1024,256]{1,0:T(8,128)(2,1)S(1)} %get-tuple-element.192), channel_id=1, source_target_pairs={{240,0},{0,16},{16,32},{32,48},{48,64},{64,80},{80,96},{96,112},{1... | collective-permute-start | bytes 1572872 | tf_op jit(solution)/shard_map/while/body/eval_jaxpr/ppermute | solution.py:13
  141.1 10.7 %collective-permute-start = (bf16[1024,256]{1,0:T(8,128)(2,1)S(1)}, bf16[1024,256]{1,0:T(8,128)(2,1)S(1)}, u32[]{:S(2)}, u32[]{:S(2)}) collective-permute-start(bf16[1024,256]{1,0:T(8,128)(2,1)S(1)} %get-tuple-element.192), channel_id=1, source_target_pairs={{240,0},{0,16},{16,32},{32,48},{48,64},{64,80},{80,96},{96,112},{1... | collective-permute-start | bytes 1572872 | tf_op jit(solution)/shard_map/while/body/eval_jaxpr/ppermute | solution.py:13
  153.2 10.7 %collective-permute-start = (bf16[1024,256]{1,0:T(8,128)(2,1)S(1)}, bf16[1024,256]{1,0:T(8,128)(2,1)S(1)}, u32[]{:S(2)}, u32[]{:S(2)}) collective-permute-start(bf16[1024,256]{1,0:T(8,128)(2,1)S(1)} %get-tuple-element.192), channel_id=1, source_target_pairs={{240,0},{0,16},{16,32},{32,48},{48,64},{64,80},{80,96},{96,112},{1... | collective-permute-start | bytes 1572872 | tf_op jit(solution)/shard_map/while/body/eval_jaxpr/ppermute | solution.py:13
  165.2 10.7 %collective-permute-start = (bf16[1024,256]{1,0:T(8,128)(2,1)S(1)}, bf16[1024,256]{1,0:T(8,128)(2,1)S(1)}, u32[]{:S(2)}, u32[]{:S(2)}) collective-permute-start(bf16[1024,256]{1,0:T(8,128)(2,1)S(1)} %get-tuple-element.192), channel_id=1, source_target_pairs={{240,0},{0,16},{16,32},{32,48},{48,64},{64,80},{80,96},{96,112},{1... | collective-permute-start | bytes 1572872 | tf_op jit(solution)/shard_map/while/body/eval_jaxpr/ppermute | solution.py:13
  177.3 10.7 %collective-permute-start = (bf16[1024,256]{1,0:T(8,128)(2,1)S(1)}, bf16[1024,256]{1,0:T(8,128)(2,1)S(1)}, u32[]{:S(2)}, u32[]{:S(2)}) collective-permute-start(bf16[1024,256]{1,0:T(8,128)(2,1)S(1)} %get-tuple-element.192), channel_id=1, source_target_pairs={{240,0},{0,16},{16,32},{32,48},{48,64},{64,80},{80,96},{96,112},{1... | collective-permute-start | bytes 1572872 | tf_op jit(solution)/shard_map/while/body/eval_jaxpr/ppermute | solution.py:13
  189.4 10.7 %collective-permute-start = (bf16[1024,256]{1,0:T(8,128)(2,1)S(1)}, bf16[1024,256]{1,0:T(8,128)(2,1)S(1)}, u32[]{:S(2)}, u32[]{:S(2)}) collective-permute-start(bf16[1024,256]{1,0:T(8,128)(2,1)S(1)} %get-tuple-element.192), channel_id=1, source_target_pairs={{240,0},{0,16},{16,32},{32,48},{48,64},{64,80},{80,96},{96,112},{1... | collective-permute-start | bytes 1572872 | tf_op jit(solution)/shard_map/while/body/eval_jaxpr/ppermute | solution.py:13
  201.5 10.7 %collective-permute-start = (bf16[1024,256]{1,0:T(8,128)(2,1)S(1)}, bf16[1024,256]{1,0:T(8,128)(2,1)S(1)}, u32[]{:S(2)}, u32[]{:S(2)}) collective-permute-start(bf16[1024,256]{1,0:T(8,128)(2,1)S(1)} %get-tuple-element.192), channel_id=1, source_target_pairs={{240,0},{0,16},{16,32},{32,48},{48,64},{64,80},{80,96},{96,112},{1... | collective-permute-start | bytes 1572872 | tf_op jit(solution)/shard_map/while/body/eval_jaxpr/ppermute | solution.py:13
  213.6 10.7 %collective-permute-start = (bf16[1024,256]{1,0:T(8,128)(2,1)S(1)}, bf16[1024,256]{1,0:T(8,128)(2,1)S(1)}, u32[]{:S(2)}, u32[]{:S(2)}) collective-permute-start(bf16[1024,256]{1,0:T(8,128)(2,1)S(1)} %get-tuple-element.192), channel_id=1, source_target_pairs={{240,0},{0,16},{16,32},{32,48},{48,64},{64,80},{80,96},{96,112},{1... | collective-permute-start | bytes 1572872 | tf_op jit(solution)/shard_map/while/body/eval_jaxpr/ppermute | solution.py:13
  225.7 10.7 %collective-permute-start = (bf16[1024,256]{1,0:T(8,128)(2,1)S(1)}, bf16[1024,256]{1,0:T(8,128)(2,1)S(1)}, u32[]{:S(2)}, u32[]{:S(2)}) collective-permute-start(bf16[1024,256]{1,0:T(8,128)(2,1)S(1)} %get-tuple-element.192), channel_id=1, source_target_pairs={{240,0},{0,16},{16,32},{32,48},{48,64},{64,80},{80,96},{96,112},{1... | collective-permute-start | bytes 1572872 | tf_op jit(solution)/shard_map/while/body/eval_jaxpr/ppermute | solution.py:13
